TPU v7x, 32 devices: a whole 2x2x4 slice. The times are simulated.
32 devices in a mesh: tile: 16 (over z, y, x), vec: 2 (over core).
Axes of the slice: x: 2, y: 2, z: 4, core: 2. Of those that a mesh axis runs over, the one named last changes fastest.
Arguments:
- trial: bfloat16 [1, 1024, 1024], P(None, ('tile', 'vec')), may hold values from -0.005859375 to 0.005859375
- psi_v: bfloat16 [1024, 8192], P(None, 'tile'), may hold values from -6 to 6
- psi_c: bfloat16 [1024, 2, 4096], P(None, 'vec', 'tile'), may hold values from -6 to 6
- screened: float32 [8192, 8192], P('tile', 'vec'), may hold values from -0.0007324219 to 0.0007324219
Outputs:
- result: float32 [1, 1024, 1024], P(None, ('tile', 'vec'))
All inputs are finite; a program needn't handle non-finite values.
Results may differ from a plain program's by a relative error of at most 0.0041.
Values may be sent and summed in bfloat16 or wider, within the bound.
A program may use at most 64 MiB of HBM per device.

v0:
```python
import jax
import jax.numpy as jnp
from jax import lax
from jax.sharding import PartitionSpec as P


def back_product(weighted_flat, panel):
    return lax.dot_general(
        weighted_flat, panel, (((1,), (1,)), ((), ())), preferred_element_type=jnp.float32
    )


def shards(trial, psi_v, psi_c, screened):
    count = trial.shape[0]
    points = psi_v.shape[1]
    conduct = trial.shape[2]
    whole = lax.all_gather(trial, ("tile", "vec"), axis=1, tiled=True)
    projected = jnp.einsum("vp,kvc->kpc", psi_v, whole, preferred_element_type=jnp.float32).astype(
        jnp.bfloat16
    )
    flat = projected.reshape(count * points, conduct)
    panel_local = psi_c[:, 0, :]
    panel = lax.all_gather(panel_local, "tile", axis=1, tiled=True)
    pair = jnp.dot(flat, panel, preferred_element_type=jnp.float32)
    weighted = (screened[None] * pair.reshape(count, points, -1)).astype(jnp.bfloat16)
    weighted_flat = weighted.reshape(count * points, -1)
    back = back_product(weighted_flat, panel)
    back = back.reshape(count, points, conduct)
    left = psi_v.astype(jnp.float32)
    summed = lax.psum(back, "vec")
    tiles = lax.axis_size("tile")
    halves = lax.axis_size("vec")
    owned = left.shape[0] // (tiles * halves)
    grouped = left.reshape(tiles, halves, owned, points)
    mine = lax.dynamic_index_in_dim(grouped, lax.axis_index("vec"), 1, keepdims=False).reshape(
        tiles * owned, points
    )
    term = jnp.dot(mine, summed[0], precision=lax.Precision.HIGHEST)
    pieces = [lax.psum_scatter(term, "tile", scatter_dimension=0, tiled=True)]
    return jnp.stack(pieces, axis=0)


def solution(mesh):
    in_specs = (
        P(None, ("tile", "vec"), None),
        P(None, "tile"),
        P(None, "vec", "tile"),
        P("tile", "vec"),
    )
    out_specs = P(None, ("tile", "vec"), None)
    return jax.shard_map(shards, mesh=mesh, in_specs=in_specs, out_specs=out_specs, check_vma=False)
```

profile of v0, /device:TPU:0, one launch (start us, length us, event | category | flops | bytes accessed | tf_op | source)
XLA Modules:
  0.0 337.5 jit_solution(1279460065863230614)
XLA Ops:
  6.5 0.0 copy-start
  6.5 0.0 all-gather.4.cloned.1.call-start
  6.5 0.7 all-gather.4.cloned.1.call-update
  7.3 0.0 all-gather.6.cloned.1.call-start
  7.3 0.7 all-gather.6.cloned.1.call-update
  8.0 0.0 all-reduce.2.cloned.1.call-start
  8.1 61.1 %all-gather.4.cloned.1.call-done = bf16[1,1024,1024]{2,1,0:T(8,128)(2,1)} async-done(((bf16[1,32,1024]{2,1,0:T(8,128)(2,1)}), bf16[1,1024,1024]{2,1,0:T(8,128)(2,1)}) %all-gather.4.cloned.1.call-update) | async-done | bytes 2097168 | tf_op jit(solution)/shard_map/all_gather | solution.py:17
  69.1 0.0 copy-done
  69.1 2.9 fusion.13
  72.0 133.2 %all-gather.6.cloned.1.call-done = bf16[1024,1,4096]{2,0,1:T(8,128)(2,1)} async-done(((bf16[1024,1,256]{2,0,1:T(8,128)(2,1)}), bf16[1024,1,4096]{2,0,1:T(8,128)(2,1)}) %all-gather.6.cloned.1.call-update) | async-done | bytes 8388624 | tf_op jit(solution)/shard_map/all_gather | solution.py:23
  205.2 18.4 %fusion = f32[512,1024]{1,0:T(8,128)} fusion(bf16[1024,1,4096]{2,0,1:T(8,128)(2,1)} %all-gather.6.cloned.1.call-done, f32[512,4096]{1,0:T(8,128)} %param.7, bf16[512,1024]{0,1:T(8,128)(2,1)S(1)} %fusion.13), kind=kOutput, calls=%fused_computation | convolution fusion | flops 8594128896 | bytes 19922944 | tf_op jit(solution)/shard_map/dot_general | solution.py:8
  223.6 0.0 all-reduce.2.cloned.1.call-update
  223.7 0.0 reduce-scatter.2.cloned.1.call-start
  223.8 19.5 %all-reduce.2.cloned.1.call-done = f32[512,1024]{1,0:T(8,128)} async-done(((f32[512,1024]{1,0:T(8,128)}), f32[512,1024]{1,0:T(8,128)}) %all-reduce.2.cloned.1.call-update) | async-done | bytes 2097168 | tf_op jit(solution)/shard_map/psum | solution.py:30
  243.3 4.8 %fusion.16 = f32[512,1024]{1,0:T(8,128)} fusion(bf16[512,512]{1,0:T(8,128)(2,1)S(1)} %bitcast.30, f32[512,1024]{1,0:T(8,128)} %all-reduce.2.cloned.1.call-done), kind=kOutput, calls=%fused_computation.10 | convolution fusion | flops 3221225472 | bytes 4718592 | tf_op jit(solution)/shard_map/dot_general | solution.py:38
  248.1 0.0 reduce-scatter.2.cloned.1.call-update
  248.1 82.8 %reduce-scatter.2.cloned.1.call-done = f32[32,1024]{1,0:T(8,128)} async-done(((f32[512,1024]{1,0:T(8,128)}), f32[32,1024]{1,0:T(8,128)}) %reduce-scatter.2.cloned.1.call-update) | async-done | bytes 131088 | tf_op jit(solution)/shard_map/reduce_scatter | solution.py:39
  (1 shorter events, 0.0 us)
Async XLA Ops:
  6.5 62.6 %copy-start = (bf16[1024,512]{1,0:T(8,128)(2,1)S(1)}, bf16[1024,512]{1,0:T(8,128)(2,1)}, u32[]{:S(2)}) copy-start(bf16[1024,512]{1,0:T(8,128)(2,1)} %param.5) | copy-start | bytes 3145732
  6.5 62.6 %all-gather.4.cloned.1.call-start = ((), (), s32[]{:S(2)}) async-start(), calls=%async_computation.1 | async-start | bytes 2162688 | tf_op jit(solution)/shard_map/all_gather | solution.py:17
  7.3 198.0 %all-gather.6.cloned.1.call-start = ((), (), s32[]{:S(2)}) async-start(), calls=%async_computation.4 | async-start | bytes 8912896 | tf_op jit(solution)/shard_map/all_gather | solution.py:23
  8.0 235.3 %all-reduce.2.cloned.1.call-start = ((), (), s32[]{:S(2)}) async-start(), calls=%async_computation.2 | async-start | bytes 4194304 | tf_op jit(solution)/shard_map/psum | solution.py:30
  223.7 107.3 %reduce-scatter.2.cloned.1.call-start = ((), (), s32[]{:S(2)}) async-start(), calls=%async_computation.3 | async-start | bytes 2228224 | tf_op jit(solution)/shard_map/reduce_scatter | solution.py:39
Sparse Core Ops, SparseCore 0:
  10.2 58.9 all-gather.3
  71.9 133.3 all-gather.5
  223.8 19.4 all-reduce.1
  248.2 82.6 reduce-scatter.1
where the time goes:
time: 338 us; the launch traced here: 337 us
  waiting for transfers between devices  298 us (88%)
  matrix products  26.1 us (8%)
  between operations  13.1 us (4%)
    all_gather x1, waiting for transfers between devices, shards(): panel = lax.all_gather(panel_local, 'tile', axis=1, tiled=True)  133 us
    reduce_scatter x1, waiting for transfers between devices, shards(): pieces = [lax.psum_scatter(term, 'tile', scatter_dimension=0, tiled=True)]  82.8 us
    all_gather x1, waiting for transfers between devices, shards(): whole = lax.all_gather(trial, ('tile', 'vec'), axis=1, tiled=True)  61.1 us
    psum x1, waiting for transfers between devices, shards(): summed = lax.psum(back, 'vec')  19.5 us
    dot_general x1, matrix products, back_product(): lax.dot_general(weighted_flat, panel, (((1,), (1,)), ((), ())), preferred...  18.4 us
  transfers between devices with their start and end apart: 4, of which 4 were waited for; matrix products, arithmetic and copies ran while one was open for 1% of the time, Pallas kernels for 0%

commit v1 on v0

--- a/solution.py
+++ b/solution.py
@@ -1,7 +1,15 @@
+import functools
+
 import jax
 import jax.numpy as jnp
 from jax import lax
+from jax.experimental import pallas as pl
+from jax.experimental.pallas import tpu as pltpu
 from jax.sharding import PartitionSpec as P
+
+RING = 4
+CUTS = 2
+EARLY = 4
 
 
 def back_product(weighted_flat, panel):
@@ -10,7 +18,7 @@
     )
 
 
-def shards(trial, psi_v, psi_c, screened):
+def plain(trial, psi_v, psi_c, screened):
     count = trial.shape[0]
     points = psi_v.shape[1]
     conduct = trial.shape[2]
@@ -35,12 +43,351 @@
     mine = lax.dynamic_index_in_dim(grouped, lax.axis_index("vec"), 1, keepdims=False).reshape(
         tiles * owned, points
     )
-    term = jnp.dot(mine, summed[0], precision=lax.Precision.HIGHEST)
-    pieces = [lax.psum_scatter(term, "tile", scatter_dimension=0, tiled=True)]
+    pieces = []
+    for one in range(count):
+        term = jnp.dot(mine, summed[one], precision=lax.Precision.HIGHEST)
+        pieces.append(lax.psum_scatter(term, "tile", scatter_dimension=0, tiled=True))
     return jnp.stack(pieces, axis=0)
 
 
+def gray(r):
+    return r + (r // 2) - 2 * (r // 3)
+
+
+def arrivals(layers):
+    near = [d for d in range(1, layers)]
+    near.sort(key=lambda d: min(d, layers - d))
+    order = [(0, 0)]
+    first = near[:2]
+    order += [(d, 0) for d in first]
+    order += [(0, 1), (0, 3)]
+    order += [(d, 0) for d in near[2:]]
+    for d in near:
+        order += [(d, 1), (d, 3)]
+    order += [(d, 2) for d in [0] + near]
+    return order
+
+
+def body(
+    tiles,
+    trial_ref,
+    psi_v_hbm,
+    psi_c_ref,
+    screened_hbm,
+    out_ref,
+    whole,
+    psi_v,
+    psi_t,
+    screened,
+    panel,
+    flat,
+    back,
+    give,
+    take,
+    term,
+    parts,
+    local_sem,
+    trial_send,
+    trial_recv,
+    hand_send,
+    hand_recv,
+    block_send,
+    block_recv,
+    back_sem,
+    part_send,
+    part_recv,
+):
+    layers = tiles // RING
+    me = lax.axis_index("tile")
+    half = lax.axis_index("vec")
+    other = 1 - half
+    a = me // RING
+    r = gray(me % RING)
+    order = arrivals(layers)
+    slot = {event: i for i, event in enumerate(order)}
+
+    def at(da, dr):
+        return ((a + da) % layers) * RING + gray((r + dr) % RING)
+
+    ahead, behind = at(0, 1), at(0, RING - 1)
+
+    def remote(src, dst, send, recv, tile, vec):
+        return pltpu.make_async_remote_copy(
+            src_ref=src,
+            dst_ref=dst,
+            send_sem=send,
+            recv_sem=recv,
+            device_id=(tile, vec),
+            device_id_type=pl.DeviceIdType.MESH,
+        )
+
+    load_psi = pltpu.make_async_copy(psi_v_hbm, psi_v, local_sem.at[0])
+    load_psi.start()
+    load_screened = pltpu.make_async_copy(screened_hbm, screened, local_sem.at[1])
+    load_screened.start()
+
+    barrier = pltpu.get_barrier_semaphore()
+    for d in range(1, tiles):
+        for v in range(2):
+            pl.semaphore_signal(
+                barrier,
+                inc=1,
+                device_id=((me + d) % tiles, v),
+                device_id_type=pl.DeviceIdType.MESH,
+            )
+    pl.semaphore_signal(
+        barrier, inc=1, device_id=(me, other), device_id_type=pl.DeviceIdType.MESH
+    )
+    pl.semaphore_wait(barrier, 2 * tiles - 1)
+
+    rows = trial_ref.shape[0]
+
+    def lines(tile, vec):
+        start = pl.multiple_of((tile * 2 + vec) * rows, rows)
+        return whole.at[pl.ds(start, rows), :]
+
+    sent = []
+    def hand(d, src):
+        tile = (me + tiles - d) % tiles
+        copy = remote(src, lines(tile, half), hand_send.at[d], hand_recv.at[d], me, other)
+        copy.start()
+        sent.append(copy)
+
+    for d in range(1, tiles):
+        copy = remote(
+            trial_ref,
+            lines(me, half),
+            trial_send.at[d],
+            trial_recv.at[d],
+            (me + d) % tiles,
+            half,
+        )
+        copy.start()
+        sent.append(copy)
+    hand(0, trial_ref)
+
+    height = psi_c_ref.shape[0] // CUTS
+    counter = [0]
+
+    def piece(ref, s):
+        return ref.at[pl.ds(s * height, height), :]
+
+    def send_block(event, s, src, owner, tile):
+        copy = remote(
+            piece(src, s),
+            piece(panel.at[owner], s),
+            block_send.at[counter[0]],
+            block_recv.at[slot[event], s],
+            tile,
+            half,
+        )
+        counter[0] += 1
+        copy.start()
+
+    for s in range(CUTS):
+        send_block((0, 1), s, psi_c_ref, me, ahead)
+        send_block((0, 3), s, psi_c_ref, me, behind)
+        for da in range(1, layers):
+            send_block((da, 0), s, psi_c_ref, me, at(da, 0))
+
+    def owner_of(event):
+        da, dr = event
+        return at(layers - da, RING - dr)
+
+    owners = {event: owner_of(event) for event in order}
+
+    def arrive(event):
+        da, dr = event
+        owner = owners[event]
+        for s in range(CUTS):
+            ref = piece(panel.at[owner], s)
+            remote(
+                ref, ref, block_send.at[0], block_recv.at[slot[event], s], me, other
+            ).wait_recv()
+            if dr == 0:
+                send_block((da, 1), s, panel.at[owner], owner, ahead)
+                send_block((da, 3), s, panel.at[owner], owner, behind)
+            elif dr == 1 and da % 2 == 0:
+                send_block((da, 2), s, panel.at[owner], owner, ahead)
+            elif dr == 3 and da % 2 == 1:
+                send_block((da, 2), s, panel.at[owner], owner, behind)
+
+    whole[pl.ds(pl.multiple_of((me * 2 + half) * rows, rows), rows), :] = trial_ref[...]
+    panel[pl.ds(me, 1)] = psi_c_ref[...][None]
+    back[...] = jnp.zeros_like(back)
+    load_psi.wait()
+    psi_t[...] = psi_v[...].T
+
+    for d in range(1, tiles):
+        tile = (me + tiles - d) % tiles
+        ref = lines(tile, half)
+        remote(ref, ref, trial_send.at[0], trial_recv.at[d], me, other).wait_recv()
+        hand(d, ref)
+    early = min(EARLY, len(order) - 1)
+    for event in order[1 : early + 1]:
+        arrive(event)
+    for d in range(tiles):
+        tile = (me + tiles - d) % tiles
+        ref = lines(tile, other)
+        remote(ref, ref, hand_send.at[0], hand_recv.at[d], me, other).wait_recv()
+
+    conduct = whole.shape[1]
+    wide = 256
+
+    def project(j, carry):
+        columns = pl.ds(pl.multiple_of(j * wide, wide), wide)
+        flat[:, columns] = jnp.dot(
+            psi_t[...], whole[:, columns], preferred_element_type=jnp.float32
+        ).astype(jnp.bfloat16)
+        return carry
+
+    lax.fori_loop(0, conduct // wide, project, 0)
+    load_screened.wait()
+
+    width = psi_c_ref.shape[1]
+    middle = conduct // 2
+
+    def use(k, carry):
+        owner = me
+        for i, event in enumerate(order):
+            if i > early:
+
+                @pl.when(k == i)
+                def _(event=event):
+                    arrive(event)
+
+            owner = jnp.where(k == i, owners[event], owner)
+        block = panel.at[owner]
+        pair = jnp.dot(flat[...], block[...], preferred_element_type=jnp.float32)
+        columns = pl.ds(pl.multiple_of(owner * width, 128), width)
+        weighted = (screened[:, columns] * pair).astype(jnp.bfloat16)
+        for h in range(2):
+            back[h] += back_product(weighted, block[pl.ds(h * middle, middle), :])
+        return carry
+
+    lax.fori_loop(0, tiles, use, 0)
+
+    give[...] = back[other].astype(jnp.bfloat16)
+    swap = remote(give, take, back_sem.at[0], back_sem.at[1], me, other)
+    swap.start()
+    swap.wait()
+    total = back[half] + take[...].astype(jnp.float32)
+    high = total.astype(jnp.bfloat16)
+    low = (total - high.astype(jnp.float32)).astype(jnp.bfloat16)
+    flat[:, :middle] = high
+    flat[:, middle:] = low
+    span = 2 * rows
+    step = psi_v.shape[0] // 4
+
+    def finish(j, carry):
+        lines_of = pl.ds(pl.multiple_of(j * step, step), step)
+        left = psi_v[lines_of, :]
+        term[lines_of, :] = (
+            jnp.dot(left, flat[:, :middle], preferred_element_type=jnp.float32)
+            + jnp.dot(left, flat[:, middle:], preferred_element_type=jnp.float32)
+        ).astype(jnp.bfloat16)
+        return carry
+
+    lax.fori_loop(0, 4, finish, 0)
+
+    def owned(tile, vec):
+        return pl.ds(pl.multiple_of(tile * span + vec * rows, rows), rows)
+
+    for d in list(range(1, tiles)) + [0]:
+        for flip in range(2):
+            if d == 0 and flip == 0:
+                continue
+            tile = (me + d) % tiles
+            vec = (half + flip) % 2
+            copy = remote(
+                term.at[owned(tile, vec), :],
+                parts.at[me, half],
+                part_send.at[d, flip],
+                part_recv.at[d, flip],
+                tile,
+                vec,
+            )
+            copy.start()
+            sent.append(copy)
+    sums = [term[owned(me, half), :].astype(jnp.float32), None]
+    for d in [0] + list(range(1, tiles)):
+        for flip in range(2):
+            if d == 0 and flip == 0:
+                continue
+            ref = parts.at[(me + tiles - d) % tiles, (half + flip) % 2]
+            remote(ref, ref, part_send.at[0, 0], part_recv.at[d, flip], me, other).wait_recv()
+            value = ref[...].astype(jnp.float32)
+            sums[flip] = value if sums[flip] is None else sums[flip] + value
+    for flip in range(2):
+        place = (half + flip) % 2
+        out_ref[:, pl.ds(pl.multiple_of(place * middle, 128), middle)] = sums[flip]
+    for copy in sent:
+        copy.wait_send()
+    for i in range(counter[0]):
+        ref = piece(psi_c_ref, 0)
+        remote(ref, ref, block_send.at[i], block_recv.at[0, 0], me, other).wait_send()
+
+
+def fused(tiles, trial, psi_v, psi_c, screened):
+    rows, conduct = trial.shape[1:]
+    valence, points = psi_v.shape
+    width = psi_c.shape[2]
+    middle = conduct // 2
+    bf16, f32 = jnp.bfloat16, jnp.float32
+    vmem = pl.BlockSpec(memory_space=pltpu.VMEM)
+    far = pl.BlockSpec(memory_space=pl.ANY)
+    dma = pltpu.SemaphoreType.DMA
+    out = pl.pallas_call(
+        functools.partial(body, tiles),
+        out_shape=jax.ShapeDtypeStruct((rows, conduct), f32),
+        in_specs=[vmem, far, vmem, far],
+        out_specs=vmem,
+        scratch_shapes=[
+            pltpu.VMEM((valence, conduct), bf16),
+            pltpu.VMEM((valence, points), bf16),
+            pltpu.VMEM((points, valence), bf16),
+            pltpu.VMEM(screened.shape, f32),
+            pltpu.VMEM((tiles, conduct, width), bf16),
+            pltpu.VMEM((points, conduct), bf16),
+            pltpu.VMEM((2, points, middle), f32),
+            pltpu.VMEM((points, middle), bf16),
+            pltpu.VMEM((points, middle), bf16),
+            pltpu.VMEM((valence, middle), bf16),
+            pltpu.VMEM((tiles, 2, rows, middle), bf16),
+            dma((2,)),
+            dma((tiles,)),
+            dma((tiles,)),
+            dma((tiles,)),
+            dma((tiles,)),
+            dma((tiles * CUTS,)),
+            dma((tiles, CUTS)),
+            dma((2,)),
+            dma((tiles, 2)),
+            dma((tiles, 2)),
+        ],
+        compiler_params=pltpu.CompilerParams(
+            collective_id=0, has_side_effects=True, vmem_limit_bytes=58 * 1024 * 1024
+        ),
+    )(trial[0], psi_v, psi_c[:, 0, :], screened)
+    return out[None]
+
+
 def solution(mesh):
+    tiles = mesh.shape["tile"]
+
+    def shards(trial, psi_v, psi_c, screened):
+        fits = (
+            trial.shape[0] == 1
+            and mesh.shape["vec"] == 2
+            and tiles % RING == 0
+            and psi_c.shape[2] % 128 == 0
+            and trial.shape[1] % 16 == 0
+            and trial.shape[2] % 256 == 0
+        )
+        if fits:
+            return fused(tiles, trial, psi_v, psi_c, screened)
+        return plain(trial, psi_v, psi_c, screened)
+
     in_specs = (
         P(None, ("tile", "vec"), None),
         P(None, "tile"),

time: 338 us -> 148 us (0.44)
  the two profiles are of different devices: /device:TPU:0 before, /device:TPU:15 now
where the time goes in v1:
time: 148 us
  Pallas kernels  146 us (99%)
  local copies, waits for them, and re-layouts  1.57 us (1%)
    pallas_call x1, Pallas kernels, fused(): pl.pallas_call(functools.partial(body, tiles), out_shape=jax.ShapeDtypeSt...  146 us

profile of v1, /device:TPU:15, one launch (start us, length us, event | category | flops | bytes accessed | tf_op | source)
XLA Modules:
  0.0 147.9 jit_solution(11963086174112416195)
XLA Ops:
  0.0 146.3 %shard_map.46 = f32[32,1024]{1,0:T(8,128)} custom-call(bf16[32,1024]{1,0:T(8,128)(2,1)} %bitcast.5, bf16[1024,512]{1,0:T(8,128)(2,1)} %psi_v_hbm.1, bf16[1024,256]{1,0:T(8,128)(2,1)} %bitcast.4, f32[512,4096]{1,0:T(8,128)} %screened_hbm.1), custom_call_target="tpu_custom_call" | custom-call | tf_op jit(solution)/shard_map/pallas_call | solution.py:340
  146.3 1.6 %copy.6 = f32[1,32,1024]{2,1,0:T(8,128)} copy(f32[1,32,1024]{2,1,0:T(8,128)} %bitcast.3) | data formatting | bytes 262144

commit v2 on v1

--- a/solution.py
+++ b/solution.py
@@ -8,8 +8,8 @@
 from jax.sharding import PartitionSpec as P
 
 RING = 4
-CUTS = 2
-EARLY = 4
+CUTS = 4
+EARLY = 3
 
 
 def back_product(weighted_flat, panel):
@@ -54,18 +54,29 @@
     return r + (r // 2) - 2 * (r // 3)
 
 
+def flip_bits(a, mask):
+    bit = 1
+    while bit <= mask:
+        if mask & bit:
+            a = a + bit - 2 * bit * ((a // bit) % 2)
+        bit *= 2
+    return a
+
+
 def arrivals(layers):
-    near = [d for d in range(1, layers)]
-    near.sort(key=lambda d: min(d, layers - d))
+    near = [d for d in [1] + list(range(layers - 1, 1, -1)) if d < layers]
     order = [(0, 0)]
-    first = near[:2]
-    order += [(d, 0) for d in first]
+    order += [(d, 0) for d in near[:1]]
     order += [(0, 1), (0, 3)]
+    for d in near[:1]:
+        order += [(d, 3), (d, 1)]
+    order += [(d, 0) for d in near[1:2]]
+    order += [(0, 2)]
     order += [(d, 0) for d in near[2:]]
-    for d in near:
-        order += [(d, 1), (d, 3)]
-    order += [(d, 2) for d in [0] + near]
-    return order
+    for d in near[1:]:
+        order += [(d, 3), (d, 1)]
+    order += [(d, 2) for d in near]
+    return near, order
 
 
 def body(
@@ -103,12 +114,13 @@
     other = 1 - half
     a = me // RING
     r = gray(me % RING)
-    order = arrivals(layers)
+    near, order = arrivals(layers)
     slot = {event: i for i, event in enumerate(order)}
 
     def at(da, dr):
-        return ((a + da) % layers) * RING + gray((r + dr) % RING)
-
+        return flip_bits(a, da) * RING + gray((r + dr) % RING)
+
+    columns_of = {d: at(d, 0) for d in range(1, layers)}
     ahead, behind = at(0, 1), at(0, RING - 1)
 
     def remote(src, dst, send, recv, tile, vec):
@@ -146,25 +158,44 @@
         start = pl.multiple_of((tile * 2 + vec) * rows, rows)
         return whole.at[pl.ds(start, rows), :]
 
+    def owner_of(event):
+        da, dr = event
+        return at(da, (RING - dr) % RING)
+
+    owners = {event: owner_of(event) for event in order}
+
+    def targets(event):
+        da, dr = event
+        if event == (0, 0):
+            return [((0, 1), ahead), ((0, 3), behind)] + [((d, 0), at(d, 0)) for d in near]
+        if dr == 0:
+            return [((da, 1), ahead), ((da, 3), behind)]
+        if dr == 1 and da % 2 == 0:
+            return [((da, 2), ahead)]
+        if dr == 3 and da % 2 == 1:
+            return [((da, 2), behind)]
+        return []
+
     sent = []
-    def hand(d, src):
-        tile = (me + tiles - d) % tiles
-        copy = remote(src, lines(tile, half), hand_send.at[d], hand_recv.at[d], me, other)
+
+    def pass_on(event, src):
+        owner = owners[event]
+        d = slot[event]
+        for later, tile in targets(event):
+            i = slot[later]
+            copy = remote(src, lines(owner, half), trial_send.at[i], trial_recv.at[i], tile, half)
+            copy.start()
+            sent.append(copy)
+        copy = remote(src, lines(owner, half), hand_send.at[d], hand_recv.at[d], me, other)
         copy.start()
         sent.append(copy)
 
-    for d in range(1, tiles):
-        copy = remote(
-            trial_ref,
-            lines(me, half),
-            trial_send.at[d],
-            trial_recv.at[d],
-            (me + d) % tiles,
-            half,
-        )
-        copy.start()
-        sent.append(copy)
-    hand(0, trial_ref)
+    def take_rows(event):
+        ref = lines(owners[event], half)
+        remote(ref, ref, trial_send.at[0], trial_recv.at[slot[event]], me, other).wait_recv()
+        pass_on(event, ref)
+
+    pass_on((0, 0), trial_ref)
 
     height = psi_c_ref.shape[0] // CUTS
     counter = [0]
@@ -184,52 +215,48 @@
         counter[0] += 1
         copy.start()
 
-    for s in range(CUTS):
-        send_block((0, 1), s, psi_c_ref, me, ahead)
-        send_block((0, 3), s, psi_c_ref, me, behind)
-        for da in range(1, layers):
-            send_block((da, 0), s, psi_c_ref, me, at(da, 0))
-
-    def owner_of(event):
-        da, dr = event
-        return at(layers - da, RING - dr)
-
-    owners = {event: owner_of(event) for event in order}
+    for d in near:
+        for s in range(CUTS):
+            send_block((d, 0), s, psi_c_ref, me, at(d, 0))
 
     def arrive(event):
-        da, dr = event
         owner = owners[event]
         for s in range(CUTS):
             ref = piece(panel.at[owner], s)
             remote(
                 ref, ref, block_send.at[0], block_recv.at[slot[event], s], me, other
             ).wait_recv()
-            if dr == 0:
-                send_block((da, 1), s, panel.at[owner], owner, ahead)
-                send_block((da, 3), s, panel.at[owner], owner, behind)
-            elif dr == 1 and da % 2 == 0:
-                send_block((da, 2), s, panel.at[owner], owner, ahead)
-            elif dr == 3 and da % 2 == 1:
-                send_block((da, 2), s, panel.at[owner], owner, behind)
-
+            onward = targets(event)
+            if s == CUTS - 1 and event == (0, 2):
+                onward = [((d, 2), columns_of[d]) for d in near]
+            elif s == CUTS - 1 and event[0] != 0 and event[1] != 0:
+                onward = []
+            for later, tile in onward:
+                send_block(later, s, panel.at[owner], owner, tile)
+
+    early = min(EARLY, len(order) - 1)
+    for d in near:
+        take_rows((d, 0))
+    for s in range(CUTS):
+        send_block((0, 1), s, psi_c_ref, me, ahead)
+        send_block((0, 3), s, psi_c_ref, me, behind)
     whole[pl.ds(pl.multiple_of((me * 2 + half) * rows, rows), rows), :] = trial_ref[...]
     panel[pl.ds(me, 1)] = psi_c_ref[...][None]
     back[...] = jnp.zeros_like(back)
     load_psi.wait()
     psi_t[...] = psi_v[...].T
 
-    for d in range(1, tiles):
-        tile = (me + tiles - d) % tiles
-        ref = lines(tile, half)
-        remote(ref, ref, trial_send.at[0], trial_recv.at[d], me, other).wait_recv()
-        hand(d, ref)
-    early = min(EARLY, len(order) - 1)
+    for event in order[1:]:
+        if event[1] in (1, 3):
+            take_rows(event)
     for event in order[1 : early + 1]:
         arrive(event)
-    for d in range(tiles):
-        tile = (me + tiles - d) % tiles
-        ref = lines(tile, other)
-        remote(ref, ref, hand_send.at[0], hand_recv.at[d], me, other).wait_recv()
+    for event in order[1:]:
+        if event[1] == 2:
+            take_rows(event)
+    for event in order:
+        ref = lines(owners[event], other)
+        remote(ref, ref, hand_send.at[0], hand_recv.at[slot[event]], me, other).wait_recv()
 
     conduct = whole.shape[1]
     wide = 256
@@ -380,6 +407,7 @@
             trial.shape[0] == 1
             and mesh.shape["vec"] == 2
             and tiles % RING == 0
+            and (tiles & (tiles - 1)) == 0
             and psi_c.shape[2] % 128 == 0
             and trial.shape[1] % 16 == 0
             and trial.shape[2] % 256 == 0

time: 148 us -> 118 us (0.80)
  Pallas kernels: 146 us -> 117 us
    pallas_call x1, Pallas kernels: 146 us -> 117 us  [fused(): pl.pallas_call(functools.partial(body, tiles), out_shape=jax.ShapeDtypeSt...]
where the time goes in v2:
time: 118 us
  Pallas kernels  117 us (99%)
  local copies, waits for them, and re-layouts  1.57 us (1%)
    pallas_call x1, Pallas kernels, fused(): pl.pallas_call(functools.partial(body, tiles), out_shape=jax.ShapeDtypeSt...  117 us

profile of v2, /device:TPU:15, one launch (start us, length us, event | category | flops | bytes accessed | tf_op | source)
XLA Modules:
  0.0 118.3 jit_solution(16201588724485348818)
XLA Ops:
  0.0 116.7 %shard_map.46 = f32[32,1024]{1,0:T(8,128)} custom-call(bf16[32,1024]{1,0:T(8,128)(2,1)} %bitcast.5, bf16[1024,512]{1,0:T(8,128)(2,1)} %psi_v_hbm.1, bf16[1024,256]{1,0:T(8,128)(2,1)} %bitcast.4, f32[512,4096]{1,0:T(8,128)} %screened_hbm.1), custom_call_target="tpu_custom_call" | custom-call | tf_op jit(solution)/shard_map/pallas_call | solution.py:367
  116.7 1.6 %copy.6 = f32[1,32,1024]{2,1,0:T(8,128)} copy(f32[1,32,1024]{2,1,0:T(8,128)} %bitcast.3) | data formatting | bytes 262144
